TPU v7x, 128 devices: a whole 4x4x4 slice. The times are simulated.
128 devices in a mesh: expert: 32 (over z, x, core), etp: 4 (over y).
Axes of the slice: x: 4, y: 4, z: 4, core: 2. Of those that a mesh axis runs over, the one named last changes fastest.
Arguments:
- tokens: bfloat16 [16384, 2560], P(('expert', 'etp')), may hold values from -6 to 6
- routes: int32 [16384, 1], P(('expert', 'etp')), may hold values from 0 to 31; in each aligned block of 128 rows (0 to 127, 128 to 255, ...) at most 12 rows name the same one
- scores: float32 [16384], P(('expert', 'etp')), may hold values from 0.1 to 1
- gate_weight: bfloat16 [32, 2560, 4096], P('expert', None, 'etp'), may hold values from -0.125 to 0.125
- up_weight: bfloat16 [32, 2560, 4096], P('expert', None, 'etp'), may hold values from -0.125 to 0.125
- down_weight: bfloat16 [32, 4096, 2560], P('expert', 'etp'), may hold values from -0.09375 to 0.09375
Outputs:
- layer_out: bfloat16 [16384, 2560], P(('expert', 'etp'))
Inputs may be any that keep to these rules, and one draw needn't show every extreme that they name: `routes`: within each device's aligned block of 128 rows no expert is named by more than 12 rows, a bound that some block reaches; every expert is named by some row.
All inputs are finite; a program needn't handle non-finite values.
Results may differ from a plain program's by a relative error of at most 0.014.
Values may be sent and summed in bfloat16 or wider, within the bound.
A program may use at most 128 MiB of HBM per device.

v0:
```python
import jax
import jax.numpy as jnp
from jax import lax
from jax.sharding import PartitionSpec as P


def hidden_rows(row_block, gate_local, up_local):
    flattened = row_block.reshape(-1, row_block.shape[-1])
    gate_out = jnp.dot(flattened, gate_local, preferred_element_type=jnp.float32)
    up_out = jnp.dot(flattened, up_local, preferred_element_type=jnp.float32)
    hidden = (jax.nn.silu(gate_out) * up_out).astype(jnp.bfloat16)
    return hidden.reshape(row_block.shape[:-1] + (gate_local.shape[1],))


def local(tokens, routes, scores, gate_weight, up_weight, down_weight):
    experts = lax.axis_size("expert")
    tok_rows, features = tokens.shape
    slot_count = 3 * tok_rows // experts
    expert_ids = routes[:, 0]
    earlier = jnp.arange(tok_rows)[:, None] < jnp.arange(tok_rows)[None, :]
    same = expert_ids[:, None] == expert_ids[None, :]
    position = jnp.sum((same & earlier).astype(jnp.int32), axis=0, dtype=jnp.int32)
    target = expert_ids * slot_count + position
    placing = (
        target[None, :] == jnp.arange(experts * slot_count, dtype=jnp.int32)[:, None]
    ).astype(jnp.bfloat16)
    outgoing = jnp.dot(placing, tokens, preferred_element_type=jnp.float32).astype(jnp.bfloat16)
    outgoing = outgoing.reshape(experts, slot_count, features)
    gate_local = gate_weight[0]
    up_local = up_weight[0]
    down_local = down_weight[0]
    received = lax.all_to_all(outgoing, "expert", split_axis=0, concat_axis=0, tiled=True)
    grouped = lax.all_gather(
        received.reshape(experts * slot_count, features), "etp", axis=0, tiled=True
    )
    hidden = hidden_rows(grouped, gate_local, up_local)
    partial_value = jnp.dot(hidden, down_local, preferred_element_type=jnp.float32)
    partial_value = partial_value.astype(jnp.bfloat16)
    summed = lax.psum_scatter(partial_value, "etp", scatter_dimension=0, tiled=True)
    summed = lax.all_to_all(
        summed.reshape(experts, slot_count, features),
        "expert",
        split_axis=0,
        concat_axis=0,
        tiled=True,
    )
    collected = lax.dot_general(
        placing,
        summed.reshape(experts * slot_count, features),
        (((0,), (0,)), ((), ())),
        preferred_element_type=jnp.float32,
    )
    return (collected * scores[:, None]).astype(jnp.bfloat16)


def solution(mesh):
    in_specs = (
        P(("expert", "etp"), None),
        P(("expert", "etp"), None),
        P(("expert", "etp")),
        P("expert", None, "etp"),
        P("expert", None, "etp"),
        P("expert", "etp", None),
    )
    out_specs = P(("expert", "etp"), None)
    return jax.shard_map(local, mesh=mesh, in_specs=in_specs, out_specs=out_specs, check_vma=False)
```

profile of v0, /device:TPU:1, one launch (start us, length us, event | category | flops | bytes accessed | tf_op | source)
XLA Modules:
  0.0 308.4 jit_solution(9060369646275938181)
XLA Ops:
  6.5 0.0 copy-start
  6.5 0.0 all-gather.2.cloned.1.call-start
  6.5 0.8 convert_reduce_fusion
  7.4 0.7 multiply_add_fusion
  8.0 0.0 copy-done
  8.0 2.0 convolution_convert_fusion.1
  10.0 2.5 reshape.22
  12.5 43.4 %all_to_all.10 = bf16[32,12,2560]{2,1,0:T(8,128)(2,1)} all-to-all(bf16[32,12,2560]{2,1,0:T(8,128)(2,1)S(1)} %reshape.22), channel_id=1, replica_groups=mesh['expert'=32,'etp'=4] {'expert'}, dimensions={0} | all-to-all | bytes 3932160 | tf_op jit(solution)/shard_map/all_to_all | solution.py:32
  55.9 4.0 %reshape.23 = bf16[384,2560]{1,0:T(8,128)(2,1)} reshape(bf16[32,12,2560]{2,1,0:T(8,128)(2,1)} %all_to_all.10) | data formatting | bytes 3932160 | tf_op jit(solution)/shard_map/reshape | solution.py:34
  59.9 0.0 all-gather.2.cloned.1.call-update
  59.9 0.0 reduce-scatter.2.cloned.1.call-start
  60.0 76.4 %all-gather.2.cloned.1.call-done = bf16[1536,2560]{1,0:T(8,128)(2,1)} async-done(((bf16[384,2560]{1,0:T(8,128)(2,1)}), bf16[1536,2560]{1,0:T(8,128)(2,1)}) %all-gather.2.cloned.1.call-update) | async-done | bytes 7864336 | tf_op jit(solution)/shard_map/all_gather | solution.py:33
  136.4 13.8 %fusion.1 = f32[1536,1024]{1,0:T(8,128)} fusion(bf16[1536,2560]{1,0:T(8,128)(2,1)} %all-gather.2.cloned.1.call-done, bf16[1,2560,1024]{2,1,0:T(8,128)(2,1)} %param.10), kind=kOutput, calls=%fused_computation.3 | convolution fusion | flops 8053063680 | bytes 19398656 | tf_op jit(solution)/shard_map/dot_general | solution.py:10
  150.2 25.3 %convolution_convert_fusion = bf16[1536,2560]{1,0:T(8,128)(2,1)} fusion(bf16[1,1024,2560]{2,1,0:T(8,128)(2,1)} %param.11, f32[1536,1024]{1,0:T(8,128)} %fusion.1, bf16[1536,2560]{1,0:T(8,128)(2,1)} %all-gather.2.cloned.1.call-done, bf16[1,2560,1024]{2,1,0:T(8,128)(2,1)} %param.9), kind=kOutput, calls=%fused_computation | convolution fusion | flops 16119496704 | bytes 32505856 | tf_op jit(solution)/shard_map/dot_general | solution.py:37
  175.5 0.0 reduce-scatter.2.cloned.1.call-update
  175.5 77.9 %reduce-scatter.2.cloned.1.call-done = bf16[384,2560]{1,0:T(8,128)(2,1)} async-done(((bf16[1536,2560]{1,0:T(8,128)(2,1)}), bf16[384,2560]{1,0:T(8,128)(2,1)}) %reduce-scatter.2.cloned.1.call-update) | async-done | bytes 1966096 | tf_op jit(solution)/shard_map/reduce_scatter | solution.py:39
  253.5 2.5 reshape.24
  255.9 0.0 copy-start.1
  256.0 41.6 %all_to_all.11 = bf16[32,12,2560]{2,1,0:T(8,128)(2,1)} all-to-all(bf16[32,12,2560]{2,1,0:T(8,128)(2,1)S(1)} %reshape.24), channel_id=1, replica_groups=mesh['expert'=32,'etp'=4] {'expert'}, dimensions={0} | all-to-all | bytes 3932160 | tf_op jit(solution)/shard_map/all_to_all | solution.py:40
  297.5 2.7 reshape.25
  300.2 0.0 copy-done.1
  300.2 1.4 fusion.9
Async XLA Ops:
  6.5 1.5 copy-start
  6.5 129.9 %all-gather.2.cloned.1.call-start = ((), (), s32[]{:S(2)}) async-start(), calls=%async_computation.3 | async-start | bytes 9830400 | tf_op jit(solution)/shard_map/all_gather | solution.py:33
  59.9 193.5 %reduce-scatter.2.cloned.1.call-start = ((), (), s32[]{:S(2)}) async-start(), calls=%async_computation.4 | async-start | bytes 9830400 | tf_op jit(solution)/shard_map/reduce_scatter | solution.py:39
  255.9 44.2 %copy-start.1 = (f32[128]{0:T(128)S(1)}, f32[128]{0:T(128)}, u32[]{:S(2)}) copy-start(f32[128]{0:T(128)} %param.8) | copy-start | bytes 1540
Sparse Core Ops, SparseCore 0:
  60.0 76.3 all-gather.1
  175.6 77.7 reduce-scatter.1
where the time goes:
time: 309 us; the launch traced here: 308 us
  waiting for transfers between devices  154 us (50%)
  blocking collectives  84.9 us (27%)
  matrix products  42.5 us (14%)
  between operations  13.4 us (4%)
  local copies, waits for them, and re-layouts  11.7 us (4%)
    reduce_scatter x1, waiting for transfers between devices, local(): lax.psum_scatter(partial_value, 'etp', scatter_dimension=0, tiled=True)  77.9 us
    all_gather x1, waiting for transfers between devices, local(): lax.all_gather(received.reshape(experts * slot_count, features), 'etp', a...  76.4 us
    all_to_all x1, blocking collectives, local(): lax.all_to_all(outgoing, 'expert', split_axis=0, concat_axis=0, tiled=True)  43.4 us
    all_to_all x1, blocking collectives, local(): lax.all_to_all(summed.reshape(experts, slot_count, features), 'expert', s...  41.6 us
    dot_general x1, matrix products, local(): jnp.dot(hidden, down_local, preferred_element_type=jnp.float32)  25.3 us
    dot_general x1, matrix products, hidden_rows(): up_out = jnp.dot(flattened, up_local, preferred_element_type=jnp.float32)  13.8 us
  transfers between devices with their start and end apart: 2, of which 2 were waited for; matrix products, arithmetic and copies ran while one was open for 0% of the time, Pallas kernels for 0%

commit v1 on v0

--- a/solution.py
+++ b/solution.py
@@ -30,8 +30,14 @@
     up_local = up_weight[0]
     down_local = down_weight[0]
     received = lax.all_to_all(outgoing, "expert", split_axis=0, concat_axis=0, tiled=True)
-    grouped = lax.all_gather(
-        received.reshape(experts * slot_count, features), "etp", axis=0, tiled=True
+    grouped = jnp.concatenate(
+        lax.all_to_all(
+            jnp.stack([received.reshape(experts * slot_count, features)] * lax.axis_size("etp")),
+            "etp",
+            0,
+            0,
+        ),
+        axis=0,
     )
     hidden = hidden_rows(grouped, gate_local, up_local)
     partial_value = jnp.dot(hidden, down_local, preferred_element_type=jnp.float32)

time: 309 us -> 319 us (1.032)
  blocking collectives: 84.9 us -> 176 us
  waiting for transfers between devices: 154 us -> 74.3 us
  matrix products: 42.5 us -> 38.7 us
    all_to_all x0 -> x1, blocking collectives: none -> 91.4 us  [local(): lax.all_to_all(jnp.stack([received.reshape(experts * slot_count, features...]
    all_gather x1 -> x0, waiting for transfers between devices: 76.4 us -> none  [local(): lax.all_gather(received.reshape(experts * slot_count, features), 'etp', a...]
    reshape x1 -> x0, local copies, waits for them, and re-layouts: 4.04 us -> none  [local(): received.reshape(experts * slot_count, features)]
    dot_general x1, matrix products: 13.8 us -> 10.1 us  [hidden_rows(): up_out = jnp.dot(flattened, up_local, preferred_element_type=jnp.float32)]
    reduce_scatter x1, waiting for transfers between devices: 77.9 us -> 74.3 us  [local(): lax.psum_scatter(partial_value, 'etp', scatter_dimension=0, tiled=True)]
    another operation x0 -> x2, local copies, waits for them, and re-layouts: none -> 3.26 us  [local(): jnp.stack([received.reshape(experts * slot_count, features)] * lax.axis_s...]
  transfers between devices with their start and end apart: 2 -> 1, of which waited for: 2 -> 1; matrix products, arithmetic and copies ran while one was open for 0% -> 0% of each run, Pallas kernels for 0% -> 0%
where the time goes in v1:
time: 319 us; the launch traced here: 318 us
  blocking collectives  176 us (55%)
  waiting for transfers between devices  74.3 us (23%)
  matrix products  38.7 us (12%)
  local copies, waits for them, and re-layouts  14 us (4%)
  between operations  13.5 us (4%)
    all_to_all x1, blocking collectives, local(): lax.all_to_all(jnp.stack([received.reshape(experts * slot_count, features...  91.4 us
    reduce_scatter x1, waiting for transfers between devices, local(): lax.psum_scatter(partial_value, 'etp', scatter_dimension=0, tiled=True)  74.3 us
    all_to_all x1, blocking collectives, local(): lax.all_to_all(outgoing, 'expert', split_axis=0, concat_axis=0, tiled=True)  43.4 us
    all_to_all x1, blocking collectives, local(): lax.all_to_all(summed.reshape(experts, slot_count, features), 'expert', s...  41.6 us
    dot_general x1, matrix products, local(): jnp.dot(hidden, down_local, preferred_element_type=jnp.float32)  25.2 us
    dot_general x1, matrix products, hidden_rows(): up_out = jnp.dot(flattened, up_local, preferred_element_type=jnp.float32)  10.1 us
  transfers between devices with their start and end apart: 1, of which 1 were waited for; matrix products, arithmetic and copies ran while one was open for 0% of the time, Pallas kernels for 0%

profile of v1, /device:TPU:1, one launch (start us, length us, event | category | flops | bytes accessed | tf_op | source)
XLA Modules:
  0.0 318.3 jit_solution(6440138016965082301)
XLA Ops:
  6.5 0.0 copy-start
  6.5 0.0 reduce-scatter.2.cloned.1.call-start
  6.5 0.8 convert_reduce_fusion
  7.4 0.7 multiply_add_fusion
  8.0 0.0 copy-done
  8.0 2.0 convolution_convert_fusion.1
  10.0 2.5 reshape.24
  12.5 43.4 %all_to_all.15 = bf16[32,12,2560]{2,1,0:T(8,128)(2,1)} all-to-all(bf16[32,12,2560]{2,1,0:T(8,128)(2,1)S(1)} %reshape.24), channel_id=1, replica_groups=mesh['expert'=32,'etp'=4] {'expert'}, dimensions={0} | all-to-all | bytes 3932160 | tf_op jit(solution)/shard_map/all_to_all | solution.py:32
  55.8 2.7 stack_reshape.2
  58.5 0.0 slice-start
  58.5 0.6 stack.3
  59.1 0.0 slice-start.1
  59.1 91.4 %all_to_all.16 = bf16[4,384,2560]{2,1,0:T(8,128)(2,1)S(1)} all-to-all(bf16[4,384,2560]{2,1,0:T(8,128)(2,1)S(1)} %stack.3), channel_id=1, replica_groups=mesh['expert'=32,'etp'=4] {'etp'}, dimensions={0} | all-to-all | bytes 15728640 | tf_op jit(solution)/shard_map/all_to_all | solution.py:34
  150.6 3.2 copy-done.1
  153.7 0.0 slice-done
  153.7 10.1 %fusion.1 = f32[1536,1024]{1,0:T(8,128)} fusion(bf16[1536,2560]{1,0:T(8,128)(2,1)S(1)} %bitcast.20, bf16[1,2560,1024]{2,1,0:T(8,128)(2,1)S(1)} %bitcast.23), kind=kOutput, calls=%fused_computation.3 | convolution fusion | flops 8053063680 | bytes 19398656 | tf_op jit(solution)/shard_map/dot_general | solution.py:10
  163.8 25.2 %convolution_convert_fusion = bf16[1536,2560]{1,0:T(8,128)(2,1)} fusion(bf16[1,1024,2560]{2,1,0:T(8,128)(2,1)} %param.11, f32[1536,1024]{1,0:T(8,128)} %fusion.1, bf16[1536,2560]{1,0:T(8,128)(2,1)} %bitcast.21, bf16[1,2560,1024]{2,1,0:T(8,128)(2,1)} %param.9), kind=kOutput, calls=%fused_computation | convolution fusion | flops 16119496704 | bytes 32505856 | tf_op jit(solution)/shard_map/dot_general | solution.py:43
  189.1 0.0 reduce-scatter.2.cloned.1.call-update
  189.1 74.3 %reduce-scatter.2.cloned.1.call-done = bf16[384,2560]{1,0:T(8,128)(2,1)} async-done(((bf16[1536,2560]{1,0:T(8,128)(2,1)}), bf16[384,2560]{1,0:T(8,128)(2,1)}) %reduce-scatter.2.cloned.1.call-update) | async-done | bytes 1966096 | tf_op jit(solution)/shard_map/reduce_scatter | solution.py:45
  263.4 2.5 reshape.26
  265.8 0.0 copy-start.2
  265.9 41.6 %all_to_all.17 = bf16[32,12,2560]{2,1,0:T(8,128)(2,1)} all-to-all(bf16[32,12,2560]{2,1,0:T(8,128)(2,1)S(1)} %reshape.26), channel_id=1, replica_groups=mesh['expert'=32,'etp'=4] {'expert'}, dimensions={0} | all-to-all | bytes 3932160 | tf_op jit(solution)/shard_map/all_to_all | solution.py:46
  307.4 2.7 reshape.27
  310.1 1.4 fusion.9
  (4 shorter events, 0.0 us)
Async XLA Ops:
  6.5 1.5 copy-start
  6.5 256.8 %reduce-scatter.2.cloned.1.call-start = ((), (), s32[]{:S(2)}) async-start(), calls=%async_computation.4 | async-start | bytes 9830400 | tf_op jit(solution)/shard_map/reduce_scatter | solution.py:45
  58.5 95.2 %slice-start = ((s8[5242880]{0:T(1024)(128)(4,1)}), s8[4194304]{0:T(1024)(128)(4,1)S(1)}, s32[]{:S(2)}) async-start(s8[5242880]{0:T(1024)(128)(4,1)} %bitcast.22), calls=%async_computation.5 | async-start | bytes 8388608
  59.1 94.6 %slice-start.1 = ((s8[5242880]{0:T(1024)(128)(4,1)}), s8[1048576]{0:T(1024)(128)(4,1)S(1)}, s32[]{:S(2)}) async-start(s8[5242880]{0:T(1024)(128)(4,1)} %bitcast.22), calls=%async_computation.6 | async-start | bytes 2097152
  150.6 3.2 copy-start.1
  265.8 44.2 %copy-start.2 = (f32[128]{0:T(128)S(1)}, f32[128]{0:T(128)}, u32[]{:S(2)}) copy-start(f32[128]{0:T(128)} %param.8) | copy-start | bytes 1540
Sparse Core Ops, SparseCore 0:
  189.2 74.0 reduce-scatter.1
